TPU v7x, 32 devices: a whole 2x2x4 slice. The times are simulated.
32 devices in a mesh: lon: 16 (over z, x, core), mem: 2 (over y).
Axes of the slice: x: 2, y: 2, z: 4, core: 2. Of those that a mesh axis runs over, the one named last changes fastest.
Arguments:
- ensemble: bfloat16 [128, 6, 524288], P('mem', None, 'lon'), may hold values from -6 to 6
- control: float32 [128, 524288], P('mem', 'lon'), may hold values from -6 to 6
- obs_tiles: bfloat16 [2048, 128, 128], P('lon'), as said below
- innovation: float32 [2048, 128], P('lon'), may hold values from -6 to 6
- obs_weight: float32 [2048, 128], P('lon'), may hold values from 0.25 to 4
- obs_counts: int32 [2048], P('lon'), may hold values from 16 to 128, as said below
- node_blocks: int32 [2048], replicated, may hold values from 0 to 4095, as said below
- obs_slots: int32 [2048], replicated, may hold values from 0 to 5
Outputs:
- gradient: float32 [128, 524288], P('mem', 'lon')
Inputs may be any that keep to these rules, and one draw needn't show every extreme that they name: `node_blocks`: within the entries of one owner (aligned runs of 128), at most 8 name node blocks of one lon index (blocks d * 256 to (d + 1) * 256 - 1); in every draw some owner names exactly 8 of one lon index. `obs_counts`: some block in every draw is full. `obs_tiles`: each tile has a positive diagonal plus off-diagonal entries.
All inputs are finite; a program needn't handle non-finite values.
Results may differ from a plain program's by a relative error of at most 0.0003.
Values sent between devices are 32-bit elements; how exact they have to be, the bound alone decides.
A program may use at most 192 MiB of HBM per device.

v0:
```python
import functools
import math

import jax
import jax.numpy as jnp
import numpy as np
from jax import lax
from jax.experimental import pallas as pl
from jax.experimental.pallas import tpu as pltpu
from jax.sharding import PartitionSpec as P

CAP = 8
GROUP = 8
WIDE = 16
ROWS = 16
MESH = pl.DeviceIdType.MESH
F32 = jnp.float32
BF16 = jnp.bfloat16
ANY = pl.BlockSpec(memory_space=pl.ANY)
VMEM = pl.BlockSpec(memory_space=pltpu.VMEM)
SMEM = pl.BlockSpec(memory_space=pltpu.SMEM)
LIMIT = 60 << 20


def params(**kw):
    return pltpu.CompilerParams(vmem_limit_bytes=LIMIT, **kw)


def tables(blk):
    lag = np.arange(blk)[:, None] - np.arange(blk)[None, :]
    every = np.arange(-blk, blk + 1)
    norm = np.sqrt(np.sum(np.exp(-((3.0 * every / blk) ** 2))))
    parts = []
    for shift in range(3):
        cells = lag + (shift - 1) * blk
        raw = np.where(np.abs(cells) <= blk, np.exp(-0.5 * (3.0 * cells / blk) ** 2), 0.0)
        parts.append(raw / norm)
    bf = jnp.bfloat16.dtype if hasattr(jnp.bfloat16, "dtype") else np.dtype(jnp.bfloat16)

    def halves(value):
        high = value.astype(np.float32).astype(bf)
        low = (value - high.astype(np.float64)).astype(np.float32).astype(bf)
        return high, low

    high, low = halves(np.concatenate(parts, axis=0))
    forward = np.concatenate(
        [
            np.concatenate([high, low], axis=1),
            np.concatenate([high, np.zeros_like(low)], axis=1),
        ],
        axis=0,
    )
    high, low = halves(np.concatenate(parts[::-1], axis=1))
    backward = np.concatenate(
        [
            np.concatenate([high, low], axis=1),
            np.concatenate([high, np.zeros_like(low)], axis=1),
        ],
        axis=0,
    )
    return forward, backward


def split(value):
    high = value.astype(BF16)
    return high, (value - high.astype(F32)).astype(BF16)


def prepare_kernel(nb, blk, ranks, nodes_ref, slots_ref, ctrl_ref, code_ref, obs_ref, before_ref,
                   after_ref, land, sends, recvs):
    lon, obs = nodes_ref.shape
    nodes = ctrl_ref.shape[1]
    my, mm = lax.axis_index("lon"), lax.axis_index("mem")
    right, left = lax.rem(my + 1, lon), lax.rem(my + lon - 1, lon)
    barrier = pltpu.get_barrier_semaphore()
    for peer in (left, right):
        pl.semaphore_signal(barrier, inc=1, device_id=(peer, mm), device_id_type=MESH)
    pl.semaphore_wait(barrier, 2)
    copies = [
        pltpu.make_async_remote_copy(
            src_ref=ctrl_ref.at[:, pl.ds(start, blk)],
            dst_ref=land.at[side],
            send_sem=sends.at[side],
            recv_sem=recvs.at[side],
            device_id=(peer, mm),
            device_id_type=MESH,
        )
        for side, (start, peer) in enumerate(((nodes - blk, right), (0, left)))
    ]
    for copy in copies:
        copy.start()
    index_tables(nb, ranks, my, mm, nodes_ref, slots_ref, code_ref, obs_ref)
    for copy in copies:
        copy.wait()
    before_ref[...] = land[0]
    after_ref[...] = land[1]


def exchange_kernel(src_ref, out_ref, land, sends, recvs):
    count = src_ref.shape[0]
    parts = lax.axis_size("mem")
    me = lax.axis_index("lon") * parts + lax.axis_index("mem")
    barrier = pltpu.get_barrier_semaphore()

    def greet(off, carry):
        peer = lax.rem(me + off, count)
        pl.semaphore_signal(
            barrier, inc=1, device_id=(peer // parts, lax.rem(peer, parts)), device_id_type=MESH
        )
        return carry

    lax.fori_loop(1, count, greet, 0)
    pl.semaphore_wait(barrier, count - 1)

    def copy(off, peer, slot):
        return pltpu.make_async_remote_copy(
            src_ref=src_ref.at[peer],
            dst_ref=land.at[slot],
            send_sem=sends.at[off],
            recv_sem=recvs.at[off],
            device_id=(peer // parts, lax.rem(peer, parts)),
            device_id_type=MESH,
        )

    def send(off, carry):
        copy(off, lax.rem(me + off, count), me).start()
        return carry

    lax.fori_loop(1, count, send, 0)
    out_ref[pl.ds(me, 1)] = src_ref[pl.ds(me, 1)]

    def finish(off, carry):
        peer = lax.rem(me + off, count)
        source = lax.rem(me + count - off, count)
        copy(off, peer, source).wait_recv()
        out_ref[pl.ds(source, 1)] = land[pl.ds(source, 1)]
        copy(off, peer, source).wait_send()
        return carry

    lax.fori_loop(1, count, finish, 0)


def exchange(value, number):
    count = value.shape[0]
    return pl.pallas_call(
        exchange_kernel,
        out_shape=jax.ShapeDtypeStruct(value.shape, value.dtype),
        in_specs=[VMEM],
        out_specs=VMEM,
        scratch_shapes=[
            pltpu.VMEM(value.shape, value.dtype),
            pltpu.SemaphoreType.DMA((count,)),
            pltpu.SemaphoreType.DMA((count,)),
        ],
        compiler_params=pltpu.CompilerParams(collective_id=number, has_side_effects=True),
        name=f"exchange{number}",
    )(value)


def index_tables(nb, ranks, my, mm, nodes_ref, slots_ref, code_ref, obs_ref):
    lon, obs = nodes_ref.shape
    tri = (
        lax.broadcasted_iota(jnp.int32, (obs, obs), 0)
        < lax.broadcasted_iota(jnp.int32, (obs, obs), 1)
    ).astype(F32).astype(BF16)
    lane = lax.broadcasted_iota(jnp.int32, (lon, 128), 1)

    def ranked(match):
        return jnp.dot(match.astype(F32).astype(BF16), tri, preferred_element_type=F32)

    local = nodes_ref[...] - my * nb
    match = (local >= 0) & (local < nb)
    rank = ranked(match)
    value = (slots_ref[...] * nb + local + 1).astype(F32)
    code = jnp.zeros((lon, 128), F32)
    for k in range(CAP):
        hit = match & (rank == float(k))
        code = jnp.where(lane == k, jnp.sum(jnp.where(hit, value, 0.0), axis=1, keepdims=True), code)
    code_ref[...] = code.astype(jnp.int32) - 1

    base = lax.broadcasted_iota(jnp.int32, (lon, obs), 0) * nb
    mine = nodes_ref[pl.ds(my, 1), :] - base
    match = (mine >= 0) & (mine < nb)
    rank = ranked(match) - (mm * ranks).astype(F32)
    value = (lax.broadcasted_iota(jnp.int32, (lon, obs), 1) + 1).astype(F32)
    which = jnp.zeros((lon, 128), F32)
    for r in range(ranks):
        hit = match & (rank == float(r))
        which = jnp.where(lane == r, jnp.sum(jnp.where(hit, value, 0.0), axis=1, keepdims=True), which)
    obs_ref[...] = which.astype(jnp.int32) - 1


def tile_copies(code_ref, ens_ref, buf, sems, nb, blk, groups):
    def start(g, carry):
        for k in range(GROUP):
            code = jnp.maximum(code_ref[g, k], 0)
            column = pl.multiple_of((code % nb) * blk, blk)
            pltpu.make_async_copy(
                ens_ref.at[code // nb, :, pl.ds(column, blk)], buf.at[g * GROUP + k], sems.at[g]
            ).start()
        return carry

    lax.fori_loop(0, groups, start, 0)


def wait_group(buf, sems, g):
    view = buf.at[pl.ds(g * GROUP, GROUP)]
    pltpu.make_async_copy(view, view, sems.at[g]).wait()


def fetch_kernel(nb, blk, scaling, code_ref, before_ref, after_ref, table_ref, ctrl_ref, ens_ref,
                 out_ref, ext, buf, sems, row_sems):
    groups = code_ref.shape[0]
    members, nodes = ctrl_ref.shape
    chunks = members // ROWS
    copies = [
        pltpu.make_async_copy(
            ctrl_ref.at[pl.ds(i * 8, 8), :], ext.at[pl.ds(i * 8, 8), pl.ds(blk, nodes)], row_sems.at[i]
        )
        for i in range(members // 8)
    ]
    for copy in copies[: ROWS // 8]:
        copy.start()
    tile_copies(code_ref, ens_ref, buf, sems, nb, blk, groups)
    for copy in copies[ROWS // 8 :]:
        copy.start()
    ext[:, :blk] = before_ref[...]
    ext[:, nodes + blk :] = after_ref[...]
    per = WIDE // GROUP
    for c in range(chunks):
        for copy in copies[c * ROWS // 8 : (c + 1) * ROWS // 8]:
            copy.wait()
        rows = slice(c * ROWS, (c + 1) * ROWS)

        def step(i, carry):
            spots = [(i * per + j, k) for j in range(per) for k in range(GROUP)]
            pieces, live = [], []
            for g, k in spots:
                code = code_ref[g, k]
                live.append((code >= 0).astype(F32) * scaling)
                column = pl.multiple_of((jnp.maximum(code, 0) % nb) * blk, blk)
                pieces.append(ext[rows, pl.ds(column, 3 * blk)])
            high, low = split(jnp.concatenate(pieces, axis=0))
            both = jnp.dot(
                jnp.concatenate([high, low], axis=1), table_ref[...], preferred_element_type=F32
            )
            weights = both[:, :blk] + both[:, blk:]
            if c == 0:
                for j in range(per):
                    wait_group(buf, sems, i * per + j)
            for n, (g, k) in enumerate(spots):
                part = weights[n * ROWS : (n + 1) * ROWS] * buf[g * GROUP + k, rows].astype(F32)
                total = jnp.sum(part, axis=0, keepdims=True) * live[n]
                if c == 0:
                    out_ref[g, pl.ds(k, 1), :] = total
                else:
                    out_ref[g, pl.ds(k, 1), :] += total
            return carry

        lax.fori_loop(0, groups // per, step, 0)


def pair(row):
    high, low = split(row)
    index = lax.broadcasted_iota(jnp.int32, (16, row.shape[1]), 0)
    both = jnp.where(index == 0, high.astype(F32), jnp.where(index == 1, low.astype(F32), 0.0))
    return both.astype(BF16)


def observe_kernel(which_ref, counts_ref, got_ref, innov_ref, weight_ref, tiles_ref, out_ref,
                   buf, sems):
    lon, parts, ranks, blk = got_ref.shape

    def start(s, carry):
        for r in range(ranks):
            o = jnp.maximum(which_ref[s, r], 0)
            pltpu.make_async_copy(tiles_ref.at[o], buf.at[s * ranks + r], sems.at[s]).start()
        return carry

    lax.fori_loop(0, lon, start, 0)
    lane = lax.broadcasted_iota(jnp.int32, (1, blk), 1)
    together = 2 if lon % 2 == 0 else 1

    def step(i, carry):
        todo = []
        for j in range(together):
            s = i * together + j
            view = buf.at[pl.ds(s * ranks, ranks)]
            pltpu.make_async_copy(view, view, sems.at[s]).wait()
            rows = got_ref[s, 0]
            for part in range(1, parts):
                rows = rows + got_ref[s, part]
            for r in range(ranks):
                todo.append((s, r, rows[r : r + 1]))
        seen = [
            lax.dot_general(
                pair(row), buf[s * ranks + r], (((1,), (1,)), ((), ())), preferred_element_type=F32
            )
            for s, r, row in todo
        ]
        gaps = []
        for (s, r, _), value in zip(todo, seen):
            index = which_ref[s, r]
            o = jnp.maximum(index, 0)
            count = jnp.where(index >= 0, counts_ref[o], 0)
            observed = jnp.sum(value, axis=0, keepdims=True)
            gap = weight_ref[pl.ds(o, 1), :] * (observed - innov_ref[pl.ds(o, 1), :])
            gaps.append(jnp.where(lane < count, gap, 0.0))
        for (s, r, _), gap in zip(todo, gaps):
            back = jnp.dot(pair(gap), buf[s * ranks + r], preferred_element_type=F32)
            row = jnp.sum(back, axis=0, keepdims=True)
            for part in range(parts):
                out_ref[s, part, pl.ds(r, 1), :] = row
        return carry

    lax.fori_loop(0, lon // together, step, 0)


def grad_kernel(nb, blk, scaling, code_ref, adj_ref, table_ref, ctrl_ref, ens_ref, out_ref,
                low_ref, high_ref, ext, buf, sems, row_sems, out_sems):
    groups = code_ref.shape[0]
    members, nodes = ctrl_ref.shape
    chunks = members // ROWS
    copies = [
        pltpu.make_async_copy(
            ctrl_ref.at[pl.ds(i * 8, 8), :], ext.at[pl.ds(i * 8, 8), pl.ds(blk, nodes)], row_sems.at[i]
        )
        for i in range(members // 8)
    ]
    for copy in copies[: ROWS // 8]:
        copy.start()
    tile_copies(code_ref, ens_ref, buf, sems, nb, blk, groups)
    for copy in copies[ROWS // 8 :]:
        copy.start()
    ext[:, :blk] = jnp.zeros((members, blk), F32)
    ext[:, nodes + blk :] = jnp.zeros((members, blk), F32)
    per = WIDE // GROUP
    writes = []
    for c in range(chunks):
        for copy in copies[c * ROWS // 8 : (c + 1) * ROWS // 8]:
            copy.wait()
        rows = slice(c * ROWS, (c + 1) * ROWS)

        def step(i, carry):
            if c == 0:
                for j in range(per):
                    wait_group(buf, sems, i * per + j)
            spots = [(i * per + j, k) for j in range(per) for k in range(GROUP)]
            pieces = []
            for g, k in spots:
                scale = (code_ref[g, k] >= 0).astype(F32) * scaling
                row = adj_ref[g, pl.ds(k, 1), :] * scale
                pieces.append(buf[g * GROUP + k, rows].astype(F32) * row)
            high, low = split(jnp.concatenate(pieces, axis=0))
            both = jnp.dot(
                jnp.concatenate([high, low], axis=1), table_ref[...], preferred_element_type=F32
            )
            total = both[:, : 3 * blk] + both[:, 3 * blk :]
            for n, (g, k) in enumerate(spots):
                column = pl.multiple_of((jnp.maximum(code_ref[g, k], 0) % nb) * blk, blk)
                ext[rows, pl.ds(column, 3 * blk)] += total[n * ROWS : (n + 1) * ROWS]
            return carry

        lax.fori_loop(0, groups // per, step, 0)
        for i in range(c * ROWS // 8, (c + 1) * ROWS // 8):
            write = pltpu.make_async_copy(
                ext.at[pl.ds(i * 8, 8), pl.ds(blk, nodes)],
                out_ref.at[pl.ds(i * 8, 8), :],
                out_sems.at[i],
            )
            write.start()
            writes.append(write)
    low_ref[...] = ext[:, :blk]
    high_ref[...] = ext[:, nodes + blk :]
    for write in writes:
        write.wait()


def edge_kernel(blk, grad_ref, before_ref, after_ref, out_ref, first, last, sems):
    nodes = grad_ref.shape[1]
    reads = [
        pltpu.make_async_copy(grad_ref.at[:, pl.ds(0, blk)], first, sems.at[0]),
        pltpu.make_async_copy(grad_ref.at[:, pl.ds(nodes - blk, blk)], last, sems.at[1]),
    ]
    for copy in reads:
        copy.start()
    for copy in reads:
        copy.wait()
    first[...] += before_ref[...]
    last[...] += after_ref[...]
    writes = [
        pltpu.make_async_copy(first, out_ref.at[:, pl.ds(0, blk)], sems.at[0]),
        pltpu.make_async_copy(last, out_ref.at[:, pl.ds(nodes - blk, blk)], sems.at[1]),
    ]
    for copy in writes:
        copy.start()
    for copy in writes:
        copy.wait()


def local(ensemble, control, obs_tiles, innovation, obs_weight, obs_counts, node_blocks, obs_slots):
    lon, mem = lax.axis_size("lon"), lax.axis_size("mem")
    obs, blk = obs_tiles.shape[0], obs_tiles.shape[2]
    members, nodes = control.shape
    nb = nodes // blk
    ranks = CAP // mem
    scaling = 1.0 / math.sqrt(members * mem - 1)
    slots = lon * CAP
    up = [(i, (i + 1) % lon) for i in range(lon)]
    down = [(j, i) for i, j in up]
    forward, backward = tables(blk)
    ens = jnp.transpose(ensemble, (1, 0, 2))
    dma = pltpu.SemaphoreType.DMA

    code, which, before, after = pl.pallas_call(
        functools.partial(prepare_kernel, nb, blk, ranks),
        out_shape=(jax.ShapeDtypeStruct((lon, 128), jnp.int32),) * 2
        + (jax.ShapeDtypeStruct((members, blk), F32),) * 2,
        in_specs=[VMEM, VMEM, ANY],
        out_specs=(VMEM,) * 4,
        scratch_shapes=[pltpu.VMEM((2, members, blk), F32), dma((2,)), dma((2,))],
        compiler_params=pltpu.CompilerParams(collective_id=2, has_side_effects=True),
        name="prepare",
    )(node_blocks.reshape(lon, obs), obs_slots.reshape(lon, obs), control)

    part = pl.pallas_call(
        functools.partial(fetch_kernel, nb, blk, scaling),
        out_shape=jax.ShapeDtypeStruct((lon, CAP, blk), F32),
        in_specs=[SMEM, VMEM, VMEM, VMEM, ANY, ANY],
        out_specs=VMEM,
        scratch_shapes=[
            pltpu.VMEM((members, nodes + 2 * blk), F32),
            pltpu.VMEM((slots, members, blk), BF16),
            dma((lon,)),
            dma((members // 8,)),
        ],
        compiler_params=params(),
        name="fetch",
    )(code, before, after, jnp.asarray(forward), control, ens)

    got = exchange(part.reshape(lon * mem, ranks, blk), 0)
    back = pl.pallas_call(
        observe_kernel,
        out_shape=jax.ShapeDtypeStruct((lon, mem, ranks, blk), F32),
        in_specs=[SMEM, SMEM, VMEM, VMEM, VMEM, ANY],
        out_specs=VMEM,
        scratch_shapes=[pltpu.VMEM((lon * ranks, blk, blk), BF16), dma((lon,))],
        compiler_params=params(),
        name="observe",
    )(which, obs_counts, got.reshape(lon, mem, ranks, blk), innovation, obs_weight, obs_tiles)
    adj = exchange(back.reshape(lon * mem, ranks, blk), 1).reshape(lon, CAP, blk)

    table = jnp.asarray(backward)
    grad, low, high = pl.pallas_call(
        functools.partial(grad_kernel, nb, blk, scaling),
        out_shape=(jax.ShapeDtypeStruct((members, nodes), F32),)
        + (jax.ShapeDtypeStruct((members, blk), F32),) * 2,
        in_specs=[SMEM, VMEM, VMEM, ANY, ANY],
        out_specs=(ANY, VMEM, VMEM),
        scratch_shapes=[
            pltpu.VMEM((members, nodes + 2 * blk), F32),
            pltpu.VMEM((slots, members, blk), BF16),
            dma((lon,)),
            dma((members // 8,)),
            dma((members // 8,)),
        ],
        compiler_params=params(),
        name="grad",
    )(code, adj, table, control, ens)
    before = lax.ppermute(high, "lon", up)
    after = lax.ppermute(low, "lon", down)
    return pl.pallas_call(
        functools.partial(edge_kernel, blk),
        out_shape=jax.ShapeDtypeStruct((members, nodes), F32),
        in_specs=[ANY, VMEM, VMEM],
        out_specs=ANY,
        scratch_shapes=[pltpu.VMEM((members, blk), F32)] * 2 + [dma((2,))],
        input_output_aliases={0: 0},
        name="edge",
    )(grad, before, after)


def solution(mesh):
    return jax.shard_map(
        local,
        mesh=mesh,
        in_specs=(
            P("mem", None, "lon"),
            P("mem", "lon"),
            P("lon", None, None),
            P("lon", None),
            P("lon", None),
            P("lon"),
            P(),
            P(),
        ),
        out_specs=P("mem", "lon"),
        check_vma=False,
    )
```

profile of v0, /device:TPU:0, one launch (start us, length us, event | category | flops | bytes accessed | tf_op | source)
XLA Modules:
  0.0 71.1 jit_solution(7195784152741243812)
XLA Ops:
  0.0 9.3 %prepare.1 = (s32[16,128]{1,0:T(8,128)}, s32[16,128]{1,0:T(8,128)}, f32[64,128]{1,0:T(8,128)}, f32[64,128]{1,0:T(8,128)}) custom-call(s32[16,128]{1,0:T(8,128)} %bitcast.13, s32[16,128]{1,0:T(8,128)} %bitcast.14, f32[64,32768]{1,0:T(8,128)} %ctrl_ref.5), custom_call_target="tpu_custom_call" | custom-call | tf_op jit(solution)/shard_map/prepare/pallas_call | solution.py:415
  9.3 12.9 %fetch.1 = f32[16,8,128]{2,1,0:T(8,128)} custom-call(s32[16,128]{1,0:T(8,128)} %get-tuple-element.12.code_ref, f32[64,128]{1,0:T(8,128)} %get-tuple-element.14.before_ref, f32[64,128]{1,0:T(8,128)} %get-tuple-element.15.after_ref, bf16[768,256]{1,0:T(8,128)(2,1)} %constant.4.clone.table_ref, f32[64,32768]{1,0:T(8,128)} %ctrl_ref.5, bf16[6,64,32768]{2,1,0:T(8,128)(2,1)} %bitcast.7), custom_call_target="tpu_custom_call" | custom-call | tf_op jit(solution)/shard_map/fetch/pallas_call | solution.py:426
  22.3 9.8 %exchange0.1 = f32[32,4,128]{2,1,0:T(4,128)} custom-call(f32[32,4,128]{2,1,0:T(4,128)} %bitcast.10), custom_call_target="tpu_custom_call" | custom-call | tf_op jit(solution)/shard_map/exchange0/pallas_call | solution.py:145
  32.1 5.7 %observe.1 = f32[16,2,4,128]{3,2,1,0:T(4,128)} custom-call(s32[16,128]{1,0:T(8,128)} %get-tuple-element.13.which_ref, s32[128]{0:T(128)} %counts_ref.1, f32[16,2,4,128]{3,2,1,0:T(4,128)} %bitcast.11, f32[128,128]{1,0:T(8,128)} %innov_ref.1, f32[128,128]{1,0:T(8,128)} %weight_ref.1, bf16[128,128,128]{2,1,0:T(8,128)(2,1)} %tiles_ref.1), custom_call_target="tpu_custom_call" | custom-call | tf_op jit(solution)/shard_map/observe/pallas_call | solution.py:442
  37.9 9.8 %exchange1.1 = f32[32,4,128]{2,1,0:T(4,128)} custom-call(f32[32,4,128]{2,1,0:T(4,128)} %bitcast.12), custom_call_target="tpu_custom_call" | custom-call | tf_op jit(solution)/shard_map/exchange1/pallas_call | solution.py:145
  47.7 14.2 %grad.1 = (f32[64,32768]{1,0:T(8,128)}, f32[64,128]{1,0:T(8,128)}, f32[64,128]{1,0:T(8,128)}) custom-call(s32[16,128]{1,0:T(8,128)} %get-tuple-element.12.code_ref, f32[16,8,128]{2,1,0:T(8,128)} %bitcast.9, bf16[256,768]{1,0:T(8,128)(2,1)} %constant.5.clone.table_ref, f32[64,32768]{1,0:T(8,128)} %ctrl_ref.5, bf16[6,64,32768]{2,1,0:T(8,128)(2,1)} %bitcast.8), custom_call_target="tpu_custom_call" | custom-call | tf_op jit(solution)/shard_map/grad/pallas_call | solution.py:454
  61.9 0.1 collective-permute-start
  62.0 4.4 %collective-permute-start.1 = (f32[64,128]{1,0:T(8,128)}, f32[64,128]{1,0:T(8,128)S(1)}, u32[]{:S(2)}, u32[]{:S(2)}) collective-permute-start(f32[64,128]{1,0:T(8,128)} %get-tuple-element.18), channel_id=1, source_target_pairs={{2,0},{4,2},{6,4},{8,6},{10,8},{12,10},{14,12},{16,14},{18,16},{20... | collective-permute-start | bytes 98312 | tf_op jit(solution)/shard_map/ppermute | solution.py:471
  66.4 1.8 %collective-permute-done.before_ref = f32[64,128]{1,0:T(8,128)S(1)} collective-permute-done((f32[64,128]{1,0:T(8,128)}, f32[64,128]{1,0:T(8,128)S(1)}, u32[]{:S(2)}, u32[]{:S(2)}) %collective-permute-start) | collective-permute-done | bytes 32800 | tf_op jit(solution)/shard_map/ppermute | solution.py:470
  68.2 0.0 copy-start
  68.2 0.1 collective-permute-done.1.after_ref
  68.3 0.0 copy-start.1
  68.3 0.5 copy-done
  68.8 0.1 copy-done.1
  68.9 2.2 %edge.1 = f32[64,32768]{1,0:T(8,128)} custom-call(f32[64,32768]{1,0:T(8,128)} %get-tuple-element.16.grad_ref, f32[64,128]{1,0:T(8,128)} %copy-done, f32[64,128]{1,0:T(8,128)} %copy-done.1), custom_call_target="tpu_custom_call", output_to_operand_aliasing={{}: (0, {})} | custom-call | tf_op jit(solution)/shard_map/edge/pallas_call | solution.py:472
Async XLA Ops:
  61.9 6.3 %collective-permute-start = (f32[64,128]{1,0:T(8,128)}, f32[64,128]{1,0:T(8,128)S(1)}, u32[]{:S(2)}, u32[]{:S(2)}) collective-permute-start(f32[64,128]{1,0:T(8,128)} %get-tuple-element.17), channel_id=1, source_target_pairs={{0,2},{2,4},{4,6},{6,8},{8,10},{10,12},{12,14},{14,16},{16,18},{18... | collective-permute-start | bytes 98312 | tf_op jit(solution)/shard_map/ppermute | solution.py:470
  62.0 6.3 %collective-permute-start.1 = (f32[64,128]{1,0:T(8,128)}, f32[64,128]{1,0:T(8,128)S(1)}, u32[]{:S(2)}, u32[]{:S(2)}) collective-permute-start(f32[64,128]{1,0:T(8,128)} %get-tuple-element.18), channel_id=1, source_target_pairs={{2,0},{4,2},{6,4},{8,6},{10,8},{12,10},{14,12},{16,14},{18,16},{20... | collective-permute-start | bytes 98312 | tf_op jit(solution)/shard_map/ppermute | solution.py:471
  68.2 0.6 copy-start
  68.3 0.6 copy-start.1
where the time goes:
time: 71.6 us; the launch traced here: 71.1 us
  Pallas kernels  64 us (89%)
  starting transfers between devices  4.49 us (6%)
  waiting for transfers between devices  1.91 us (3%)
    pallas_call x2, Pallas kernels, exchange(): pl.pallas_call(exchange_kernel, out_shape=jax.ShapeDtypeStruct(value.shap...  19.6 us
    pallas_call x1, Pallas kernels, local(): pl.pallas_call(functools.partial(grad_kernel, nb, blk, scaling), out_shap...  14.2 us
    pallas_call x1, Pallas kernels, local(): pl.pallas_call(functools.partial(fetch_kernel, nb, blk, scaling), out_sha...  12.9 us
    pallas_call x1, Pallas kernels, local(): pl.pallas_call(functools.partial(prepare_kernel, nb, blk, ranks), out_sha...  9.33 us
    pallas_call x1, Pallas kernels, local(): pl.pallas_call(observe_kernel, out_shape=jax.ShapeDtypeStruct((lon, mem,...  5.75 us
    ppermute x1, starting transfers between devices, local(): after = lax.ppermute(low, 'lon', down)  4.39 us
    pallas_call x1, Pallas kernels, local(): pl.pallas_call(functools.partial(edge_kernel, blk), out_shape=jax.ShapeDt...  2.19 us
    ppermute x1, waiting for transfers between devices, local(): before = lax.ppermute(high, 'lon', up)  1.8 us
  transfers between devices with their start and end apart: 2, of which 2 were waited for; matrix products, arithmetic and copies ran while one was open for 0% of the time, Pallas kernels for 0%

commit v1 on v0

--- a/solution.py
+++ b/solution.py
@@ -66,8 +66,8 @@
     return high, (value - high.astype(F32)).astype(BF16)
 
 
-def prepare_kernel(nb, blk, ranks, nodes_ref, slots_ref, ctrl_ref, code_ref, obs_ref, before_ref,
-                   after_ref, land, sends, recvs):
+def prepare_kernel(nb, blk, ranks, nodes_ref, slots_ref, ctrl_ref, code_ref, slot_ref, obs_ref,
+                   before_ref, after_ref, land, sends, recvs):
     lon, obs = nodes_ref.shape
     nodes = ctrl_ref.shape[1]
     my, mm = lax.axis_index("lon"), lax.axis_index("mem")
@@ -89,7 +89,7 @@
     ]
     for copy in copies:
         copy.start()
-    index_tables(nb, ranks, my, mm, nodes_ref, slots_ref, code_ref, obs_ref)
+    index_tables(nb, blk, ranks, my, mm, nodes_ref, slots_ref, code_ref, slot_ref, obs_ref)
     for copy in copies:
         copy.wait()
     before_ref[...] = land[0]
@@ -97,47 +97,44 @@
 
 
 def exchange_kernel(src_ref, out_ref, land, sends, recvs):
-    count = src_ref.shape[0]
-    parts = lax.axis_size("mem")
-    me = lax.axis_index("lon") * parts + lax.axis_index("mem")
+    lon, mem = lax.axis_size("lon"), lax.axis_size("mem")
+    me = lax.axis_index("lon") * mem + lax.axis_index("mem")
     barrier = pltpu.get_barrier_semaphore()
 
-    def greet(off, carry):
-        peer = lax.rem(me + off, count)
-        pl.semaphore_signal(
-            barrier, inc=1, device_id=(peer // parts, lax.rem(peer, parts)), device_id_type=MESH
-        )
-        return carry
-
-    lax.fori_loop(1, count, greet, 0)
-    pl.semaphore_wait(barrier, count - 1)
-
-    def copy(off, peer, slot):
+    def others(act):
+        def step(a, carry):
+            for b in range(mem):
+                pl.when(a * mem + b != me)(functools.partial(act, a, b, a * mem + b))
+            return carry
+
+        lax.fori_loop(0, lon, step, 0)
+
+    def greet(a, b, peer):
+        pl.semaphore_signal(barrier, inc=1, device_id=(a, b), device_id_type=MESH)
+
+    def copy(a, b, peer, slot):
         return pltpu.make_async_remote_copy(
             src_ref=src_ref.at[peer],
             dst_ref=land.at[slot],
-            send_sem=sends.at[off],
-            recv_sem=recvs.at[off],
-            device_id=(peer // parts, lax.rem(peer, parts)),
+            send_sem=sends.at[peer],
+            recv_sem=recvs.at[slot],
+            device_id=(a, b),
             device_id_type=MESH,
         )
 
-    def send(off, carry):
-        copy(off, lax.rem(me + off, count), me).start()
-        return carry
-
-    lax.fori_loop(1, count, send, 0)
-    out_ref[pl.ds(me, 1)] = src_ref[pl.ds(me, 1)]
-
-    def finish(off, carry):
-        peer = lax.rem(me + off, count)
-        source = lax.rem(me + count - off, count)
-        copy(off, peer, source).wait_recv()
-        out_ref[pl.ds(source, 1)] = land[pl.ds(source, 1)]
-        copy(off, peer, source).wait_send()
-        return carry
-
-    lax.fori_loop(1, count, finish, 0)
+    def send(a, b, peer):
+        copy(a, b, peer, me).start()
+
+    def finish(a, b, peer):
+        copy(a, b, peer, peer).wait_recv()
+        copy(a, b, peer, peer).wait_send()
+
+    others(greet)
+    land[pl.ds(me, 1)] = src_ref[pl.ds(me, 1)]
+    pl.semaphore_wait(barrier, lon * mem - 1)
+    others(send)
+    others(finish)
+    out_ref[...] = land[...]
 
 
 def exchange(value, number):
@@ -157,7 +154,7 @@
     )(value)
 
 
-def index_tables(nb, ranks, my, mm, nodes_ref, slots_ref, code_ref, obs_ref):
+def index_tables(nb, blk, ranks, my, mm, nodes_ref, slots_ref, code_ref, slot_ref, obs_ref):
     lon, obs = nodes_ref.shape
     tri = (
         lax.broadcasted_iota(jnp.int32, (obs, obs), 0)
@@ -171,12 +168,20 @@
     local = nodes_ref[...] - my * nb
     match = (local >= 0) & (local < nb)
     rank = ranked(match)
-    value = (slots_ref[...] * nb + local + 1).astype(F32)
-    code = jnp.zeros((lon, 128), F32)
+    column = (local * blk).astype(F32)
+    slot = slots_ref[...].astype(F32)
+    columns = jnp.zeros((lon, 128), F32)
+    slots = jnp.zeros((lon, 128), F32)
     for k in range(CAP):
         hit = match & (rank == float(k))
-        code = jnp.where(lane == k, jnp.sum(jnp.where(hit, value, 0.0), axis=1, keepdims=True), code)
-    code_ref[...] = code.astype(jnp.int32) - 1
+        columns = jnp.where(
+            lane == k, jnp.sum(jnp.where(hit, column, 0.0), axis=1, keepdims=True), columns
+        )
+        slots = jnp.where(
+            lane == k, jnp.sum(jnp.where(hit, slot, 0.0), axis=1, keepdims=True), slots
+        )
+    code_ref[...] = columns.astype(jnp.int32)
+    slot_ref[...] = slots.astype(jnp.int32)
 
     base = lax.broadcasted_iota(jnp.int32, (lon, obs), 0) * nb
     mine = nodes_ref[pl.ds(my, 1), :] - base
@@ -190,13 +195,12 @@
     obs_ref[...] = which.astype(jnp.int32) - 1
 
 
-def tile_copies(code_ref, ens_ref, buf, sems, nb, blk, groups):
+def tile_copies(code_ref, slot_ref, ens_ref, buf, sems, blk, groups):
     def start(g, carry):
         for k in range(GROUP):
-            code = jnp.maximum(code_ref[g, k], 0)
-            column = pl.multiple_of((code % nb) * blk, blk)
+            column = pl.multiple_of(code_ref[g, k], blk)
             pltpu.make_async_copy(
-                ens_ref.at[code // nb, :, pl.ds(column, blk)], buf.at[g * GROUP + k], sems.at[g]
+                ens_ref.at[slot_ref[g, k], :, pl.ds(column, blk)], buf.at[g * GROUP + k], sems.at[g]
             ).start()
         return carry
 
@@ -208,7 +212,7 @@
     pltpu.make_async_copy(view, view, sems.at[g]).wait()
 
 
-def fetch_kernel(nb, blk, scaling, code_ref, before_ref, after_ref, table_ref, ctrl_ref, ens_ref,
+def fetch_kernel(blk, scaling, code_ref, slot_ref, before_ref, after_ref, table_ref, ctrl_ref, ens_ref,
                  out_ref, ext, buf, sems, row_sems):
     groups = code_ref.shape[0]
     members, nodes = ctrl_ref.shape
@@ -221,7 +225,7 @@
     ]
     for copy in copies[: ROWS // 8]:
         copy.start()
-    tile_copies(code_ref, ens_ref, buf, sems, nb, blk, groups)
+    tile_copies(code_ref, slot_ref, ens_ref, buf, sems, blk, groups)
     for copy in copies[ROWS // 8 :]:
         copy.start()
     ext[:, :blk] = before_ref[...]
@@ -234,11 +238,9 @@
 
         def step(i, carry):
             spots = [(i * per + j, k) for j in range(per) for k in range(GROUP)]
-            pieces, live = [], []
+            pieces = []
             for g, k in spots:
-                code = code_ref[g, k]
-                live.append((code >= 0).astype(F32) * scaling)
-                column = pl.multiple_of((jnp.maximum(code, 0) % nb) * blk, blk)
+                column = pl.multiple_of(code_ref[g, k], blk)
                 pieces.append(ext[rows, pl.ds(column, 3 * blk)])
             high, low = split(jnp.concatenate(pieces, axis=0))
             both = jnp.dot(
@@ -250,7 +252,7 @@
                     wait_group(buf, sems, i * per + j)
             for n, (g, k) in enumerate(spots):
                 part = weights[n * ROWS : (n + 1) * ROWS] * buf[g * GROUP + k, rows].astype(F32)
-                total = jnp.sum(part, axis=0, keepdims=True) * live[n]
+                total = jnp.sum(part, axis=0, keepdims=True) * scaling
                 if c == 0:
                     out_ref[g, pl.ds(k, 1), :] = total
                 else:
@@ -316,7 +318,7 @@
     lax.fori_loop(0, lon // together, step, 0)
 
 
-def grad_kernel(nb, blk, scaling, code_ref, adj_ref, table_ref, ctrl_ref, ens_ref, out_ref,
+def grad_kernel(blk, scaling, code_ref, slot_ref, adj_ref, table_ref, ctrl_ref, ens_ref, out_ref,
                 low_ref, high_ref, ext, buf, sems, row_sems, out_sems):
     groups = code_ref.shape[0]
     members, nodes = ctrl_ref.shape
@@ -329,7 +331,7 @@
     ]
     for copy in copies[: ROWS // 8]:
         copy.start()
-    tile_copies(code_ref, ens_ref, buf, sems, nb, blk, groups)
+    tile_copies(code_ref, slot_ref, ens_ref, buf, sems, blk, groups)
     for copy in copies[ROWS // 8 :]:
         copy.start()
     ext[:, :blk] = jnp.zeros((members, blk), F32)
@@ -348,8 +350,7 @@
             spots = [(i * per + j, k) for j in range(per) for k in range(GROUP)]
             pieces = []
             for g, k in spots:
-                scale = (code_ref[g, k] >= 0).astype(F32) * scaling
-                row = adj_ref[g, pl.ds(k, 1), :] * scale
+                row = adj_ref[g, pl.ds(k, 1), :] * scaling
                 pieces.append(buf[g * GROUP + k, rows].astype(F32) * row)
             high, low = split(jnp.concatenate(pieces, axis=0))
             both = jnp.dot(
@@ -357,7 +358,7 @@
             )
             total = both[:, : 3 * blk] + both[:, 3 * blk :]
             for n, (g, k) in enumerate(spots):
-                column = pl.multiple_of((jnp.maximum(code_ref[g, k], 0) % nb) * blk, blk)
+                column = pl.multiple_of(code_ref[g, k], blk)
                 ext[rows, pl.ds(column, 3 * blk)] += total[n * ROWS : (n + 1) * ROWS]
             return carry
 
@@ -412,21 +413,21 @@
     ens = jnp.transpose(ensemble, (1, 0, 2))
     dma = pltpu.SemaphoreType.DMA
 
-    code, which, before, after = pl.pallas_call(
+    code, slot, which, before, after = pl.pallas_call(
         functools.partial(prepare_kernel, nb, blk, ranks),
-        out_shape=(jax.ShapeDtypeStruct((lon, 128), jnp.int32),) * 2
+        out_shape=(jax.ShapeDtypeStruct((lon, 128), jnp.int32),) * 3
         + (jax.ShapeDtypeStruct((members, blk), F32),) * 2,
         in_specs=[VMEM, VMEM, ANY],
-        out_specs=(VMEM,) * 4,
+        out_specs=(VMEM,) * 5,
         scratch_shapes=[pltpu.VMEM((2, members, blk), F32), dma((2,)), dma((2,))],
         compiler_params=pltpu.CompilerParams(collective_id=2, has_side_effects=True),
         name="prepare",
     )(node_blocks.reshape(lon, obs), obs_slots.reshape(lon, obs), control)
 
     part = pl.pallas_call(
-        functools.partial(fetch_kernel, nb, blk, scaling),
+        functools.partial(fetch_kernel, blk, scaling),
         out_shape=jax.ShapeDtypeStruct((lon, CAP, blk), F32),
-        in_specs=[SMEM, VMEM, VMEM, VMEM, ANY, ANY],
+        in_specs=[SMEM, SMEM, VMEM, VMEM, VMEM, ANY, ANY],
         out_specs=VMEM,
         scratch_shapes=[
             pltpu.VMEM((members, nodes + 2 * blk), F32),
@@ -436,7 +437,7 @@
         ],
         compiler_params=params(),
         name="fetch",
-    )(code, before, after, jnp.asarray(forward), control, ens)
+    )(code, slot, before, after, jnp.asarray(forward), control, ens)
 
     got = exchange(part.reshape(lon * mem, ranks, blk), 0)
     back = pl.pallas_call(
@@ -452,10 +453,10 @@
 
     table = jnp.asarray(backward)
     grad, low, high = pl.pallas_call(
-        functools.partial(grad_kernel, nb, blk, scaling),
+        functools.partial(grad_kernel, blk, scaling),
         out_shape=(jax.ShapeDtypeStruct((members, nodes), F32),)
         + (jax.ShapeDtypeStruct((members, blk), F32),) * 2,
-        in_specs=[SMEM, VMEM, VMEM, ANY, ANY],
+        in_specs=[SMEM, SMEM, VMEM, VMEM, ANY, ANY],
         out_specs=(ANY, VMEM, VMEM),
         scratch_shapes=[
             pltpu.VMEM((members, nodes + 2 * blk), F32),
@@ -466,7 +467,7 @@
         ],
         compiler_params=params(),
         name="grad",
-    )(code, adj, table, control, ens)
+    )(code, slot, adj, table, control, ens)
     before = lax.ppermute(high, "lon", up)
     after = lax.ppermute(low, "lon", down)
     return pl.pallas_call(

time: 71.6 us -> 71.1 us (level)
  no operation moved by 1% of the time
where the time goes in v1:
time: 71.1 us; the launch traced here: 70.5 us
  Pallas kernels  63.4 us (89%)
  starting transfers between devices  4.49 us (6%)
  waiting for transfers between devices  1.91 us (3%)
    pallas_call x2, Pallas kernels, exchange(): pl.pallas_call(exchange_kernel, out_shape=jax.ShapeDtypeStruct(value.shap...  19 us
    pallas_call x1, Pallas kernels, local(): pl.pallas_call(functools.partial(grad_kernel, blk, scaling), out_shape=(j...  14 us
    pallas_call x1, Pallas kernels, local(): pl.pallas_call(functools.partial(fetch_kernel, blk, scaling), out_shape=j...  13.2 us
    pallas_call x1, Pallas kernels, local(): pl.pallas_call(functools.partial(prepare_kernel, nb, blk, ranks), out_sha...  9.33 us
    pallas_call x1, Pallas kernels, local(): pl.pallas_call(observe_kernel, out_shape=jax.ShapeDtypeStruct((lon, mem,...  5.75 us
    ppermute x1, starting transfers between devices, local(): after = lax.ppermute(low, 'lon', down)  4.33 us
    pallas_call x1, Pallas kernels, local(): pl.pallas_call(functools.partial(edge_kernel, blk), out_shape=jax.ShapeDt...  2.19 us
    ppermute x1, waiting for transfers between devices, local(): before = lax.ppermute(high, 'lon', up)  1.8 us
  transfers between devices with their start and end apart: 2, of which 2 were waited for; matrix products, arithmetic and copies ran while one was open for 0% of the time, Pallas kernels for 0%

profile of v1, /device:TPU:0, one launch (start us, length us, event | category | flops | bytes accessed | tf_op | source)
XLA Modules:
  0.0 70.5 jit_solution(296562469921432031)
XLA Ops:
  0.0 9.3 %prepare.1 = (s32[16,128]{1,0:T(8,128)}, s32[16,128]{1,0:T(8,128)}, s32[16,128]{1,0:T(8,128)}, f32[64,128]{1,0:T(8,128)}, f32[64,128]{1,0:T(8,128)}) custom-call(s32[16,128]{1,0:T(8,128)} %bitcast.13, s32[16,128]{1,0:T(8,128)} %bitcast.14, f32[64,32768]{1,0:T(8,128)} %ctrl_ref.5), custom_call_target="tpu_custom_call" | custom-call | tf_op jit(solution)/shard_map/prepare/pallas_call | solution.py:416
  9.3 13.2 %fetch.1 = f32[16,8,128]{2,1,0:T(8,128)} custom-call(s32[16,128]{1,0:T(8,128)} %get-tuple-element.13.code_ref, s32[16,128]{1,0:T(8,128)} %get-tuple-element.14.slot_ref, f32[64,128]{1,0:T(8,128)} %get-tuple-element.16.before_ref, f32[64,128]{1,0:T(8,128)} %get-tuple-element.17.after_ref, bf16[768,256]{1,0:T(8,128)(2,1)} %constant.4.clone.table_ref, ...), custom_call_target="tpu_custom_call" | custom-call | tf_op jit(solution)/shard_map/fetch/pallas_call | solution.py:427
  22.5 9.4 %exchange0.1 = f32[32,4,128]{2,1,0:T(4,128)} custom-call(f32[32,4,128]{2,1,0:T(4,128)} %bitcast.10), custom_call_target="tpu_custom_call" | custom-call | tf_op jit(solution)/shard_map/exchange0/pallas_call | solution.py:142
  31.9 5.7 %observe.1 = f32[16,2,4,128]{3,2,1,0:T(4,128)} custom-call(s32[16,128]{1,0:T(8,128)} %get-tuple-element.15.which_ref, s32[128]{0:T(128)} %counts_ref.1, f32[16,2,4,128]{3,2,1,0:T(4,128)} %bitcast.11, f32[128,128]{1,0:T(8,128)} %innov_ref.1, f32[128,128]{1,0:T(8,128)} %weight_ref.1, bf16[128,128,128]{2,1,0:T(8,128)(2,1)} %tiles_ref.1), custom_call_target="tpu_custom_call" | custom-call | tf_op jit(solution)/shard_map/observe/pallas_call | solution.py:443
  37.7 9.6 %exchange1.1 = f32[32,4,128]{2,1,0:T(4,128)} custom-call(f32[32,4,128]{2,1,0:T(4,128)} %bitcast.12), custom_call_target="tpu_custom_call" | custom-call | tf_op jit(solution)/shard_map/exchange1/pallas_call | solution.py:142
  47.3 14.0 %grad.1 = (f32[64,32768]{1,0:T(8,128)}, f32[64,128]{1,0:T(8,128)}, f32[64,128]{1,0:T(8,128)}) custom-call(s32[16,128]{1,0:T(8,128)} %get-tuple-element.13.code_ref, s32[16,128]{1,0:T(8,128)} %get-tuple-element.14.slot_ref, f32[16,8,128]{2,1,0:T(8,128)} %bitcast.9, bf16[256,768]{1,0:T(8,128)(2,1)} %constant.5.clone.table_ref, f32[64,32768]{1,0:T(8,128)} %ctrl_ref.5, ...), custom_call_target="tpu_custom_call" | custom-call | tf_op jit(solution)/shard_map/grad/pallas_call | solution.py:455
  61.3 0.2 collective-permute-start
  61.4 4.3 %collective-permute-start.1 = (f32[64,128]{1,0:T(8,128)}, f32[64,128]{1,0:T(8,128)S(1)}, u32[]{:S(2)}, u32[]{:S(2)}) collective-permute-start(f32[64,128]{1,0:T(8,128)} %get-tuple-element.20), channel_id=1, source_target_pairs={{2,0},{4,2},{6,4},{8,6},{10,8},{12,10},{14,12},{16,14},{18,16},{20... | collective-permute-start | bytes 98312 | tf_op jit(solution)/shard_map/ppermute | solution.py:472
  65.8 1.8 %collective-permute-done.before_ref = f32[64,128]{1,0:T(8,128)S(1)} collective-permute-done((f32[64,128]{1,0:T(8,128)}, f32[64,128]{1,0:T(8,128)S(1)}, u32[]{:S(2)}, u32[]{:S(2)}) %collective-permute-start) | collective-permute-done | bytes 32800 | tf_op jit(solution)/shard_map/ppermute | solution.py:471
  67.6 0.0 copy-start
  67.6 0.1 collective-permute-done.1.after_ref
  67.7 0.0 copy-start.1
  67.7 0.5 copy-done
  68.2 0.1 copy-done.1
  68.3 2.2 %edge.1 = f32[64,32768]{1,0:T(8,128)} custom-call(f32[64,32768]{1,0:T(8,128)} %get-tuple-element.18.grad_ref, f32[64,128]{1,0:T(8,128)} %copy-done, f32[64,128]{1,0:T(8,128)} %copy-done.1), custom_call_target="tpu_custom_call", output_to_operand_aliasing={{}: (0, {})} | custom-call | tf_op jit(solution)/shard_map/edge/pallas_call | solution.py:473
Async XLA Ops:
  61.3 6.3 %collective-permute-start = (f32[64,128]{1,0:T(8,128)}, f32[64,128]{1,0:T(8,128)S(1)}, u32[]{:S(2)}, u32[]{:S(2)}) collective-permute-start(f32[64,128]{1,0:T(8,128)} %get-tuple-element.19), channel_id=1, source_target_pairs={{0,2},{2,4},{4,6},{6,8},{8,10},{10,12},{12,14},{14,16},{16,18},{18... | collective-permute-start | bytes 98312 | tf_op jit(solution)/shard_map/ppermute | solution.py:471
  61.4 6.2 %collective-permute-start.1 = (f32[64,128]{1,0:T(8,128)}, f32[64,128]{1,0:T(8,128)S(1)}, u32[]{:S(2)}, u32[]{:S(2)}) collective-permute-start(f32[64,128]{1,0:T(8,128)} %get-tuple-element.20), channel_id=1, source_target_pairs={{2,0},{4,2},{6,4},{8,6},{10,8},{12,10},{14,12},{16,14},{18,16},{20... | collective-permute-start | bytes 98312 | tf_op jit(solution)/shard_map/ppermute | solution.py:472
  67.6 0.6 copy-start
  67.7 0.6 copy-start.1

commit v2 on v1

--- a/solution.py
+++ b/solution.py
@@ -11,7 +11,8 @@
 
 CAP = 8
 GROUP = 8
-WIDE = 16
+WIDE = 32
+WIDE_FETCH = 64
 ROWS = 16
 MESH = pl.DeviceIdType.MESH
 F32 = jnp.float32
@@ -230,7 +231,7 @@
         copy.start()
     ext[:, :blk] = before_ref[...]
     ext[:, nodes + blk :] = after_ref[...]
-    per = WIDE // GROUP
+    per = WIDE_FETCH // GROUP
     for c in range(chunks):
         for copy in copies[c * ROWS // 8 : (c + 1) * ROWS // 8]:
             copy.wait()

time: 71.1 us -> 64 us (0.900)
  Pallas kernels: 63.4 us -> 56.4 us
    pallas_call x1, Pallas kernels: 13.2 us -> 8.69 us  [local(): pl.pallas_call(functools.partial(fetch_kernel, blk, scaling), out_shape=j...]
    pallas_call x1, Pallas kernels: 14 us -> 11.4 us  [local(): pl.pallas_call(functools.partial(grad_kernel, blk, scaling), out_shape=(j...]
where the time goes in v2:
time: 64 us; the launch traced here: 63.4 us
  Pallas kernels  56.4 us (88%)
  starting transfers between devices  4.49 us (7%)
  waiting for transfers between devices  1.91 us (3%)
    pallas_call x2, Pallas kernels, exchange(): pl.pallas_call(exchange_kernel, out_shape=jax.ShapeDtypeStruct(value.shap...  19 us
    pallas_call x1, Pallas kernels, local(): pl.pallas_call(functools.partial(grad_kernel, blk, scaling), out_shape=(j...  11.4 us
    pallas_call x1, Pallas kernels, local(): pl.pallas_call(functools.partial(prepare_kernel, nb, blk, ranks), out_sha...  9.33 us
    pallas_call x1, Pallas kernels, local(): pl.pallas_call(functools.partial(fetch_kernel, blk, scaling), out_shape=j...  8.69 us
    pallas_call x1, Pallas kernels, local(): pl.pallas_call(observe_kernel, out_shape=jax.ShapeDtypeStruct((lon, mem,...  5.75 us
    ppermute x1, starting transfers between devices, local(): after = lax.ppermute(low, 'lon', down)  4.36 us
    pallas_call x1, Pallas kernels, local(): pl.pallas_call(functools.partial(edge_kernel, blk), out_shape=jax.ShapeDt...  2.19 us
    ppermute x1, waiting for transfers between devices, local(): before = lax.ppermute(high, 'lon', up)  1.8 us
  transfers between devices with their start and end apart: 2, of which 2 were waited for; matrix products, arithmetic and copies ran while one was open for 0% of the time, Pallas kernels for 0%

profile of v2, /device:TPU:0, one launch (start us, length us, event | category | flops | bytes accessed | tf_op | source)
XLA Modules:
  0.0 63.4 jit_solution(14492131847524674916)
XLA Ops:
  0.0 9.3 %prepare.1 = (s32[16,128]{1,0:T(8,128)}, s32[16,128]{1,0:T(8,128)}, s32[16,128]{1,0:T(8,128)}, f32[64,128]{1,0:T(8,128)}, f32[64,128]{1,0:T(8,128)}) custom-call(s32[16,128]{1,0:T(8,128)} %bitcast.13, s32[16,128]{1,0:T(8,128)} %bitcast.14, f32[64,32768]{1,0:T(8,128)} %ctrl_ref.5), custom_call_target="tpu_custom_call" | custom-call | tf_op jit(solution)/shard_map/prepare/pallas_call | solution.py:417
  9.3 8.7 %fetch.1 = f32[16,8,128]{2,1,0:T(8,128)} custom-call(s32[16,128]{1,0:T(8,128)} %get-tuple-element.13.code_ref, s32[16,128]{1,0:T(8,128)} %get-tuple-element.14.slot_ref, f32[64,128]{1,0:T(8,128)} %get-tuple-element.16.before_ref, f32[64,128]{1,0:T(8,128)} %get-tuple-element.17.after_ref, bf16[768,256]{1,0:T(8,128)(2,1)} %constant.4.clone.table_ref, ...), custom_call_target="tpu_custom_call" | custom-call | tf_op jit(solution)/shard_map/fetch/pallas_call | solution.py:428
  18.0 9.4 %exchange0.1 = f32[32,4,128]{2,1,0:T(4,128)} custom-call(f32[32,4,128]{2,1,0:T(4,128)} %bitcast.10), custom_call_target="tpu_custom_call" | custom-call | tf_op jit(solution)/shard_map/exchange0/pallas_call | solution.py:143
  27.5 5.7 %observe.1 = f32[16,2,4,128]{3,2,1,0:T(4,128)} custom-call(s32[16,128]{1,0:T(8,128)} %get-tuple-element.15.which_ref, s32[128]{0:T(128)} %counts_ref.1, f32[16,2,4,128]{3,2,1,0:T(4,128)} %bitcast.11, f32[128,128]{1,0:T(8,128)} %innov_ref.1, f32[128,128]{1,0:T(8,128)} %weight_ref.1, bf16[128,128,128]{2,1,0:T(8,128)(2,1)} %tiles_ref.1), custom_call_target="tpu_custom_call" | custom-call | tf_op jit(solution)/shard_map/observe/pallas_call | solution.py:444
  33.2 9.6 %exchange1.1 = f32[32,4,128]{2,1,0:T(4,128)} custom-call(f32[32,4,128]{2,1,0:T(4,128)} %bitcast.12), custom_call_target="tpu_custom_call" | custom-call | tf_op jit(solution)/shard_map/exchange1/pallas_call | solution.py:143
  42.8 11.4 %grad.1 = (f32[64,32768]{1,0:T(8,128)}, f32[64,128]{1,0:T(8,128)}, f32[64,128]{1,0:T(8,128)}) custom-call(s32[16,128]{1,0:T(8,128)} %get-tuple-element.13.code_ref, s32[16,128]{1,0:T(8,128)} %get-tuple-element.14.slot_ref, f32[16,8,128]{2,1,0:T(8,128)} %bitcast.9, bf16[256,768]{1,0:T(8,128)(2,1)} %constant.5.clone.table_ref, f32[64,32768]{1,0:T(8,128)} %ctrl_ref.5, ...), custom_call_target="tpu_custom_call" | custom-call | tf_op jit(solution)/shard_map/grad/pallas_call | solution.py:456
  54.2 0.1 collective-permute-start
  54.4 4.4 %collective-permute-start.1 = (f32[64,128]{1,0:T(8,128)}, f32[64,128]{1,0:T(8,128)S(1)}, u32[]{:S(2)}, u32[]{:S(2)}) collective-permute-start(f32[64,128]{1,0:T(8,128)} %get-tuple-element.20), channel_id=1, source_target_pairs={{2,0},{4,2},{6,4},{8,6},{10,8},{12,10},{14,12},{16,14},{18,16},{20... | collective-permute-start | bytes 98312 | tf_op jit(solution)/shard_map/ppermute | solution.py:473
  58.7 1.8 %collective-permute-done.before_ref = f32[64,128]{1,0:T(8,128)S(1)} collective-permute-done((f32[64,128]{1,0:T(8,128)}, f32[64,128]{1,0:T(8,128)S(1)}, u32[]{:S(2)}, u32[]{:S(2)}) %collective-permute-start) | collective-permute-done | bytes 32800 | tf_op jit(solution)/shard_map/ppermute | solution.py:472
  60.5 0.0 copy-start
  60.5 0.1 collective-permute-done.1.after_ref
  60.6 0.0 copy-start.1
  60.6 0.5 copy-done
  61.1 0.1 copy-done.1
  61.2 2.2 %edge.1 = f32[64,32768]{1,0:T(8,128)} custom-call(f32[64,32768]{1,0:T(8,128)} %get-tuple-element.18.grad_ref, f32[64,128]{1,0:T(8,128)} %copy-done, f32[64,128]{1,0:T(8,128)} %copy-done.1), custom_call_target="tpu_custom_call", output_to_operand_aliasing={{}: (0, {})} | custom-call | tf_op jit(solution)/shard_map/edge/pallas_call | solution.py:474
Async XLA Ops:
  54.2 6.3 %collective-permute-start = (f32[64,128]{1,0:T(8,128)}, f32[64,128]{1,0:T(8,128)S(1)}, u32[]{:S(2)}, u32[]{:S(2)}) collective-permute-start(f32[64,128]{1,0:T(8,128)} %get-tuple-element.19), channel_id=1, source_target_pairs={{0,2},{2,4},{4,6},{6,8},{8,10},{10,12},{12,14},{14,16},{16,18},{18... | collective-permute-start | bytes 98312 | tf_op jit(solution)/shard_map/ppermute | solution.py:472
  54.4 6.3 %collective-permute-start.1 = (f32[64,128]{1,0:T(8,128)}, f32[64,128]{1,0:T(8,128)S(1)}, u32[]{:S(2)}, u32[]{:S(2)}) collective-permute-start(f32[64,128]{1,0:T(8,128)} %get-tuple-element.20), channel_id=1, source_target_pairs={{2,0},{4,2},{6,4},{8,6},{10,8},{12,10},{14,12},{16,14},{18,16},{20... | collective-permute-start | bytes 98312 | tf_op jit(solution)/shard_map/ppermute | solution.py:473
  60.5 0.6 copy-start
  60.6 0.6 copy-start.1
